TPU v7x, 32 devices: a whole 2x2x4 slice. The times are simulated.
32 devices in a mesh: seq: 8 (over z, x), vocab: 4 (over y, core).
Axes of the slice: x: 2, y: 2, z: 4, core: 2. Of those that a mesh axis runs over, the one named last changes fastest.
Arguments:
- hidden: bfloat16 [2, 1024, 2048], P(None, 'seq'), may hold values from -6 to 6
- embedded: bfloat16 [2, 1024, 2048], P(None, 'seq'), may hold values from -6 to 6
- targets: int32 [2, 1024], P(None, 'seq'), may hold values from 0 to 51199
- main_mask: int32 [2, 1024], P(None, 'seq'), may hold values 0 or 1
- mtp_mask: int32 [2, 1024], P(None, 'seq'), may hold values from 0 to 1, as said below
- lengths: int32 [2], replicated, may hold values from 256 to 1024, as said below
- head_weight: bfloat16 [2048, 51200], P(None, ('seq', 'vocab')), may hold values from -7.6733202 to 7.6733202
- projection: bfloat16 [4096, 2048], P(None, 'vocab'), may hold values from -0.09375 to 0.09375
- main_gain: float32 [2048], replicated, may hold values from 0.5 to 1.5
- hidden_gain: float32 [2048], replicated, may hold values from 0.5 to 1.5
- embed_gain: float32 [2048], replicated, may hold values from 0.5 to 1.5
- mtp_gain: float32 [2048], replicated, may hold values from 0.5 to 1.5
Outputs:
- main_tokens: float32 [2, 1024], P(None, 'seq')
- mtp_tokens: float32 [2, 1024], P(None, 'seq')
- total_loss: float32 [], replicated
Inputs may be any that keep to these rules, and one draw needn't show every extreme that they name: `mtp_mask`: 1 at every position that is a multiple of 128. `lengths`: the first sequence has length 1024.
All inputs are finite; a program needn't handle non-finite values. No bound on the sum of `main_mask` on one device may be relied on, other than what follows from the above.
Results may differ from a plain program's by a relative error of at most 0.0004.
The roundings to bfloat16 on the way count: a program that leaves them out, or rounds other values in their place, can miss the bound.
Values may be sent and summed in bfloat16 or wider, within the bound.
A program may use at most 128 MiB of HBM per device.

v0:
```python
import jax
import jax.numpy as jnp
from jax import lax
from jax.sharding import PartitionSpec as P

EPSILON = 1e-06
MTP_WEIGHT = 0.3


def from_behind(block, axis, distance):
    devices = range(lax.axis_size(axis))
    route = [(i - distance, i) for i in devices if i - distance in devices]
    return lax.ppermute(block, axis, route)


def partner_2(value, axis, apart):
    mask = 2**apart
    pairs = [(source, source ^ mask) for source in range(lax.axis_size(axis))]
    return lax.ppermute(value, axis, pairs)


def normalize(values, gain_vec):
    values = values.astype(jnp.float32)
    mean_square = jnp.mean(values * values, axis=-1, keepdims=True)
    return values * lax.rsqrt(mean_square + EPSILON) * gain_vec


def column_stats(logits, column_ids, wanted):
    highest = jnp.max(logits, axis=1)
    exp_total = jnp.sum(jnp.exp(logits - highest[:, None]), axis=1)
    picked = jnp.sum(jnp.where(column_ids[None, :] == wanted[:, None], logits, 0.0), axis=1)
    return (highest, exp_total, picked)


def join_stats(earlier, latter):
    highest = jnp.maximum(earlier[0], latter[0])
    exp_total = earlier[1] * jnp.exp(earlier[0] - highest) + latter[1] * jnp.exp(
        latter[0] - highest
    )
    return (highest, exp_total, earlier[2] + latter[2])


def shards(
    hidden,
    embedded,
    targets,
    main_mask,
    mtp_mask,
    lengths,
    head_weight,
    projection,
    main_gain,
    hidden_gain,
    embed_gain,
    mtp_gain,
):
    batches, seq_len, model_width = hidden.shape
    seq_index = lax.axis_index("seq")
    vocab_index = lax.axis_index("vocab")
    vocab_count = lax.axis_size("vocab")
    block_cols = head_weight.shape[1]
    positions = seq_index * seq_len + lax.broadcasted_iota(jnp.int32, (batches, seq_len), 1)
    length_col = lengths[:, None]
    keep_main = ((main_mask == 1) & (positions + 1 < length_col)).astype(jnp.float32)
    keep_mtp = ((mtp_mask == 1) & (positions >= 1) & (positions + 1 < length_col)).astype(
        jnp.float32
    )
    count_main = jnp.sum(keep_main)
    count_mtp = jnp.sum(keep_mtp)
    counted = lax.psum((count_main, count_mtp), "seq")
    main_rows = normalize(hidden, main_gain).astype(jnp.bfloat16).reshape(-1, model_width)
    incoming = from_behind(hidden[:, seq_len - 1 :, :], "seq", 1)
    previous = jnp.concatenate([incoming, hidden[:, : seq_len - 1, :]], axis=1)
    joined = jnp.concatenate(
        [normalize(previous, hidden_gain), normalize(embedded, embed_gain)], axis=2
    )
    joined = joined.astype(jnp.bfloat16).reshape(-1, 2 * model_width)
    partial_value = jnp.dot(joined, projection, preferred_element_type=jnp.float32).astype(
        jnp.bfloat16
    )
    mixed = lax.all_gather(partial_value, "vocab", axis=1, tiled=True)
    mtp_rows = normalize(mixed, mtp_gain).astype(jnp.bfloat16)
    all_rows = jnp.concatenate([main_rows, mtp_rows], axis=0)
    flat_targets = targets.reshape(-1)
    wanted = jnp.concatenate([flat_targets, flat_targets], axis=0)
    held_cols = head_weight
    levels = lax.axis_size("seq").bit_length() - 1
    for bit_number in range(1, levels):
        received = partner_2(held_cols, "seq", bit_number)
        upper_half = seq_index >> bit_number & 1 == 1
        held_cols = jnp.where(
            upper_half,
            jnp.concatenate([received, held_cols], axis=1),
            jnp.concatenate([held_cols, received], axis=1),
        )
    partner = partner_2(all_rows, "seq", 0)
    partner_wanted = partner_2(wanted, "seq", 0)
    column_pos = lax.broadcasted_iota(jnp.int32, (held_cols.shape[1],), 0)
    anchor_seq = (seq_index & 1) + 2 * (column_pos // block_cols)
    column_ids = (anchor_seq * vocab_count + vocab_index) * block_cols + column_pos % block_cols
    logits = jnp.dot(
        jnp.concatenate([all_rows, partner], axis=0), held_cols, preferred_element_type=jnp.float32
    )
    row_count = all_rows.shape[0]
    own_stats = column_stats(logits[:row_count], column_ids, wanted)
    peer_stats = column_stats(logits[row_count:], column_ids, partner_wanted)
    returned = partner_2((peer_stats[0], peer_stats[1], peer_stats[2]), "seq", 0)
    highest, exp_total, picked = join_stats(own_stats, returned)
    global_max = lax.pmax(highest, "vocab")
    global_total, target_logit = lax.psum(
        (exp_total * jnp.exp(highest - global_max), picked), "vocab"
    )
    losses = global_max + jnp.log(global_total) - target_logit
    half_rows = batches * seq_len
    main_tokens = keep_main * losses[:half_rows].reshape(batches, seq_len)
    mtp_tokens = keep_mtp * losses[half_rows:].reshape(batches, seq_len)
    main_sum = jnp.sum(main_tokens)
    mtp_sum = jnp.sum(mtp_tokens)
    summed = lax.psum((main_sum, mtp_sum), "seq")
    total_main, total_mtp = summed
    kept_main, kept_mtp = counted
    total_loss = total_main / jnp.maximum(kept_main, 1.0) + MTP_WEIGHT * total_mtp / jnp.maximum(
        kept_mtp, 1.0
    )
    return (main_tokens, mtp_tokens, total_loss)


def solution(mesh):
    return jax.shard_map(
        shards,
        mesh=mesh,
        in_specs=(
            P(None, "seq", None),
            P(None, "seq", None),
            P(None, "seq"),
            P(None, "seq"),
            P(None, "seq"),
            P(),
            P(None, ("seq", "vocab")),
            P(None, "vocab"),
            P(),
            P(),
            P(),
            P(),
        ),
        out_specs=(P(None, "seq"), P(None, "seq"), P()),
        check_vma=False,
    )
```

profile of v0, /device:TPU:0, one launch (start us, length us, event | category | flops | bytes accessed | tf_op | source)
XLA Modules:
  0.0 926.5 jit_solution(852602479931637078)
XLA Ops:
  7.2 3.1 collective-permute-start.2
  10.3 141.4 %collective-permute-done.2 = bf16[2048,1600]{0,1:T(8,128)(2,1)} collective-permute-done((bf16[2048,1600]{0,1:T(8,128)(2,1)}, bf16[2048,1600]{0,1:T(8,128)(2,1)}, u32[]{:S(2)}, u32[]{:S(2)}) %collective-permute-start.2) | collective-permute-done | bytes 6553632 | tf_op jit(solution)/shard_map/ppermute | solution.py:19
  151.8 15.6 %maximum_select_fusion.2 = bf16[2048,3200]{0,1:T(8,128)(2,1)} fusion(bf16[2048,1600]{0,1:T(8,128)(2,1)} %param.18, bf16[2048,1600]{0,1:T(8,128)(2,1)} %collective-permute-done.2, pred[]{:T(512)S(6)} %eq.40), kind=kLoop, calls=%fused_computation.8 | loop fusion | flops 58982400 | bytes 26214400 | tf_op jit(solution)/shard_map/jit(_where)/select_n | solution.py:91
  167.4 2.8 collective-permute-start.3
  170.2 3.4 collective-permute-start
  174.3 0.8 collective-permute-done
  176.1 2.0 fusion.27
  178.8 573.8 %all-gather.2.cloned.1.call-done = bf16[256,2048]{1,0:T(8,128)(2,1)} async-done(((bf16[256,512]{1,0:T(8,128)(2,1)}), bf16[256,2048]{1,0:T(8,128)(2,1)}) %all-gather.2.cloned.1.call-update) | async-done | bytes 1048592 | tf_op jit(solution)/shard_map/all_gather | solution.py:81
  752.6 1.5 fusion.18
  754.1 1.5 fusion.20
  755.6 1.5 pad_maximum_fusion
  757.1 1.5 collective-permute-start.1
  759.3 45.9 %collective-permute-done.1 = bf16[512,2048]{1,0:T(8,128)(2,1)} collective-permute-done((bf16[512,2048]{1,0:T(8,128)(2,1)}, bf16[512,2048]{1,0:T(8,128)(2,1)}, u32[]{:S(2)}, u32[]{:S(2)}) %collective-permute-start.1) | collective-permute-done | bytes 2097184 | tf_op jit(solution)/shard_map/ppermute | solution.py:19
  805.2 49.2 %fusion = f32[1024,6400]{1,0:T(8,128)} fusion(bf16[2048,3200]{0,1:T(8,128)(2,1)} %maximum_select_fusion.2, bf16[2048,3200]{0,1:T(8,128)(2,1)} %collective-permute-done.3, pred[]{:T(512)S(6)} %eq.39, bf16[512,2048]{1,0:T(8,128)(2,1)} %collective-permute-done.1, bf16[256,2048]{1,0:T(8,128)(2,1)S(1)} %fusion.20, bf16[256,2048]{1,0:T(8,128)(2,1)S(1)} %bitcast.22), kind=kOutput, calls=%fused_computation.1 | convolution fusion | flops 26974093312 | bytes 56623104 | tf_op jit(solution)/shard_map/dot_general | solution.py:101
  854.4 9.4 %slice_reduce_fusion = (f32[512]{0:T(512)S(1)}, f32[512]{0:T(512)S(1)}) fusion(f32[1024,6400]{1,0:T(8,128)} %fusion), kind=kLoop, calls=%fused_computation.13 | loop fusion | flops 6552576 | bytes 26218496 | tf_op jit(solution)/shard_map/reduce_max | solution.py:29
  863.8 1.5 collective-permute-start.4
  865.4 5.0 copy-done
  870.4 6.9 exponential_reduce_fusion.1
  877.3 1.5 collective-permute-start.7
  880.2 0.8 collective-permute-done.7
  881.0 5.7 pmax.7
  886.7 5.8 all-reduce.1
  892.5 1.2 fusion.47
  893.7 22.3 %all-reduce = (f32[]{:T(128)}, f32[]{:T(128)}, f32[]{:T(128)}, f32[]{:T(128)}) all-reduce(f32[]{:T(128)} %get-tuple-element.25, f32[]{:T(128)} %get-tuple-element.27, f32[]{:T(128)} %get-tuple-element.19, f32[]{:T(128)} %get-tuple-element.17), channel_id=1, replica_groups=mesh['seq'=8,'vocab'=4] {'seq'}, use_global_device_ids=true, to_apply=%region_14.15 | all-reduce | flops 4 | bytes 32 | tf_op jit(solution)/shard_map/psum | solution.py:119
  (52 shorter events, 4.3 us)
Async XLA Ops:
  7.2 745.4 %all-gather.2.cloned.1.call-start = ((), (), s32[]{:S(2)}) async-start(), calls=%async_computation | async-start | bytes 1310720 | tf_op jit(solution)/shard_map/all_gather | solution.py:81
  7.2 144.6 %collective-permute-start.2 = (bf16[2048,1600]{0,1:T(8,128)(2,1)}, bf16[2048,1600]{0,1:T(8,128)(2,1)}, u32[]{:S(2)}, u32[]{:S(2)}) collective-permute-start(bf16[2048,1600]{0,1:T(8,128)(2,1)} %param.18), channel_id=1, source_target_pairs={{0,8},{4,12},{8,0},{12,4},{16,24},{20,28},{24,16},{28,20},{1,9},{5... | collective-permute-start | bytes 19660808 | tf_op jit(solution)/shard_map/ppermute | solution.py:19
  10.3 159.9 %copy-start.1 = (bf16[2,128,2048]{2,1,0:T(8,128)(2,1)S(1)}, bf16[2,128,2048]{2,1,0:T(8,128)(2,1)}, u32[]{:S(2)}) copy-start(bf16[2,128,2048]{2,1,0:T(8,128)(2,1)} %param.12) | copy-start | bytes 3145732
  10.3 163.3 %copy-start.2 = (bf16[2,128,2048]{2,1,0:T(8,128)(2,1)S(1)}, bf16[2,128,2048]{2,1,0:T(8,128)(2,1)}, u32[]{:S(2)}) copy-start(bf16[2,128,2048]{2,1,0:T(8,128)(2,1)} %param.13) | copy-start | bytes 3145732
  10.3 163.6 %copy-start.3 = (f32[2048]{0:T(1024)S(1)}, f32[2048]{0:T(1024)}, u32[]{:S(2)}) copy-start(f32[2048]{0:T(1024)} %param.22) | copy-start | bytes 24580
  167.4 8.4 copy-start.4
  167.4 8.7 copy-start.11
  167.4 637.8 %collective-permute-start.3 = (bf16[2048,3200]{0,1:T(8,128)(2,1)}, bf16[2048,3200]{0,1:T(8,128)(2,1)}, u32[]{:S(2)}, u32[]{:S(2)}) collective-permute-start(bf16[2048,3200]{0,1:T(8,128)(2,1)} %maximum_select_fusion.2), channel_id=1, source_target_pairs={{0,16},{4,20},{8,24},{12,28},{16,0},{20,4},{24,8},{28,12},{1,17},{... | collective-permute-start | bytes 39321608 | tf_op jit(solution)/shard_map/ppermute | solution.py:19
  170.2 4.8 collective-permute-start
  175.9 2.6 copy-start.5
  176.1 578.0 %copy-start.6 = (f32[2048]{0:T(1024)S(1)}, f32[2048]{0:T(1024)}, u32[]{:S(2)}) copy-start(f32[2048]{0:T(1024)} %param.23) | copy-start | bytes 24580
  178.1 580.5 %copy-start.7 = (s32[2,128]{1,0:T(2,128)S(1)}, s32[2,128]{1,0:T(2,128)}, u32[]{:S(2)}) copy-start(s32[2,128]{1,0:T(2,128)} %param.14) | copy-start | bytes 3076
  757.1 48.1 %collective-permute-start.1 = (bf16[512,2048]{1,0:T(8,128)(2,1)}, bf16[512,2048]{1,0:T(8,128)(2,1)}, u32[]{:S(2)}, u32[]{:S(2)}) collective-permute-start(bf16[512,2048]{1,0:T(8,128)(2,1)} %pad_maximum_fusion), channel_id=1, source_target_pairs={{0,4},{4,0},{8,12},{12,8},{16,20},{20,16},{24,28},{28,24},{1,5},{5... | collective-permute-start | bytes 6291464 | tf_op jit(solution)/shard_map/ppermute | solution.py:19
  758.6 106.7 %collective-permute-start.6 = (s32[512]{0:T(512)S(1)}, s32[512]{0:T(512)S(1)}, u32[]{:S(2)}, u32[]{:S(2)}) collective-permute-start(s32[512]{0:T(512)S(1)} %pad_add_fusion), channel_id=1, source_target_pairs={{0,4},{4,0},{8,12},{12,8},{16,20},{20,16},{24,28},{28,24},{1,5},{5... | collective-permute-start | bytes 6152 | tf_op jit(solution)/shard_map/ppermute | solution.py:19
  854.4 16.0 %copy-start = (f32[1024,6400]{1,0:T(8,128)S(1)}, f32[1024,6400]{1,0:T(8,128)}, u32[]{:S(2)}) copy-start(f32[1024,6400]{1,0:T(8,128)} %fusion) | copy-start | bytes 78643200
  863.8 16.3 %collective-permute-start.4 = (f32[512]{0:T(512)S(1)}, f32[512]{0:T(512)S(1)}, u32[]{:S(2)}, u32[]{:S(2)}) collective-permute-start(f32[512]{0:T(512)S(1)} %get-tuple-element.9), channel_id=1, source_target_pairs={{0,4},{4,0},{8,12},{12,8},{16,20},{20,16},{24,28},{28,24},{1,5},{5... | collective-permute-start | bytes 6152 | tf_op jit(solution)/shard_map/ppermute | solution.py:19
  870.4 8.4 copy-start.8
  870.4 8.4 copy-start.9
  870.4 8.4 copy-start.10
  877.3 3.6 collective-permute-start.7
  879.6 7.1 collective-permute-start.5
Sparse Core Ops, SparseCore 0:
  178.3 574.2 all-gather.1
where the time goes:
time: 927 us; the launch traced here: 926 us
  waiting for transfers between devices  763 us (82%)
  matrix products  51.1 us (6%)
  other arithmetic  40.7 us (4%)
  blocking collectives  33.8 us (4%)
  between operations  17.9 us (2%)
  starting transfers between devices  15.1 us (2%)
    all_gather x1, waiting for transfers between devices, shards(): mixed = lax.all_gather(partial_value, 'vocab', axis=1, tiled=True)  574 us
    ppermute x7, waiting for transfers between devices, partner_2(): return lax.ppermute(value, axis, pairs)  188 us
    dot_general x1, matrix products, shards(): jnp.dot(jnp.concatenate([all_rows, partner], axis=0), held_cols, preferre...  49.2 us
    psum x1, blocking collectives, shards(): summed = lax.psum((main_sum, mtp_sum), 'seq')  22.3 us
  transfers between devices with their start and end apart: 9, of which 5 were waited for; matrix products, arithmetic and copies ran while one was open for 8% of the time, Pallas kernels for 0%

commit v1 on v0

--- a/solution.py
+++ b/solution.py
@@ -1,3 +1,4 @@
+import functools
 import jax
 import jax.numpy as jnp
 from jax import lax
@@ -5,6 +6,23 @@
 
 EPSILON = 1e-06
 MTP_WEIGHT = 0.3
+
+
+def rates_start(mine, bus_axis, ndim_at):
+    n_chips = lax.axis_size(bus_axis)
+    windows = [mine]
+    for u in range(n_chips - 1):
+        windows.append(
+            lax.ppermute(windows[-1], bus_axis, [(ii, (ii + 1) % n_chips) for ii in range(n_chips)])
+        )
+    return jnp.roll(
+        jnp.concatenate(windows[::-1], ndim_at),
+        (lax.axis_index(bus_axis) + 1) * mine.shape[ndim_at],
+        ndim_at,
+    )
+
+
+recover_the_spots = functools.partial(rates_start, bus_axis="vocab", ndim_at=1)
 
 
 def from_behind(block, axis, distance):
@@ -78,7 +96,7 @@
     partial_value = jnp.dot(joined, projection, preferred_element_type=jnp.float32).astype(
         jnp.bfloat16
     )
-    mixed = lax.all_gather(partial_value, "vocab", axis=1, tiled=True)
+    mixed = recover_the_spots(partial_value)
     mtp_rows = normalize(mixed, mtp_gain).astype(jnp.bfloat16)
     all_rows = jnp.concatenate([main_rows, mtp_rows], axis=0)
     flat_targets = targets.reshape(-1)

time: 927 us -> 907 us (0.978)
  waiting for transfers between devices: 763 us -> 417 us
  starting transfers between devices: 15.1 us -> 290 us
  blocking collectives: 33.8 us -> 100 us
  between operations: 17.9 us -> 4.59 us
    all_gather x1 -> x0, waiting for transfers between devices: 574 us -> none  [shards(): mixed = lax.all_gather(partial_value, 'vocab', axis=1, tiled=True)]
    ppermute x7, starting transfers between devices: 11.6 us -> 286 us  [partner_2(): return lax.ppermute(value, axis, pairs)]
    ppermute x7, waiting for transfers between devices: 188 us -> 400 us  [partner_2(): return lax.ppermute(value, axis, pairs)]
    psum x1, blocking collectives: 22.3 us -> 88 us  [shards(): summed = lax.psum((main_sum, mtp_sum), 'seq')]
    ppermute x0 -> x3, waiting for transfers between devices: none -> 16.7 us  [rates_start(): lax.ppermute(windows[-1], bus_axis, [(ii, (ii + 1) % n_chips) for ii in r...]
  transfers between devices with their start and end apart: 9 -> 11, of which waited for: 5 -> 8; matrix products, arithmetic and copies ran while one was open for 8% -> 8% of each run, Pallas kernels for 0% -> 0%
where the time goes in v1:
time: 907 us; the launch traced here: 906 us
  waiting for transfers between devices  417 us (46%)
  starting transfers between devices  290 us (32%)
  blocking collectives  100 us (11%)
  matrix products  50.4 us (6%)
  other arithmetic  38.3 us (4%)
    ppermute x7, waiting for transfers between devices, partner_2(): return lax.ppermute(value, axis, pairs)  400 us
    ppermute x7, starting transfers between devices, partner_2(): return lax.ppermute(value, axis, pairs)  286 us
    psum x1, blocking collectives, shards(): summed = lax.psum((main_sum, mtp_sum), 'seq')  88 us
    dot_general x1, matrix products, shards(): jnp.dot(jnp.concatenate([all_rows, partner], axis=0), held_cols, preferre...  49.2 us
  transfers between devices with their start and end apart: 11, of which 8 were waited for; matrix products, arithmetic and copies ran while one was open for 8% of the time, Pallas kernels for 0%

profile of v1, /device:TPU:0, one launch (start us, length us, event | category | flops | bytes accessed | tf_op | source)
XLA Modules:
  0.0 906.5 jit_solution(5907065701774851470)
XLA Ops:
  0.6 3.1 collective-permute-start.5
  3.8 141.4 %collective-permute-done.5 = bf16[2048,1600]{0,1:T(8,128)(2,1)} collective-permute-done((bf16[2048,1600]{0,1:T(8,128)(2,1)}, bf16[2048,1600]{0,1:T(8,128)(2,1)}, u32[]{:S(2)}, u32[]{:S(2)}) %collective-permute-start.5) | collective-permute-done | bytes 6553632 | tf_op jit(solution)/shard_map/ppermute | solution.py:37
  145.2 15.6 %maximum_select_fusion.2 = bf16[2048,3200]{0,1:T(8,128)(2,1)} fusion(bf16[2048,1600]{0,1:T(8,128)(2,1)} %param.18, bf16[2048,1600]{0,1:T(8,128)(2,1)} %collective-permute-done.5, pred[]{:T(512)S(6)} %eq.43), kind=kLoop, calls=%fused_computation.8 | loop fusion | flops 58982400 | bytes 26214400 | tf_op jit(solution)/shard_map/jit(_where)/select_n | solution.py:109
  160.8 2.8 collective-permute-start.6
  163.6 3.4 collective-permute-start
  169.8 1.2 fusion.27
  171.2 5.8 collective-permute-done.1
  177.3 5.5 collective-permute-done.2
  183.1 5.5 collective-permute-done.3
  189.4 1.5 pad_maximum_fusion
  190.9 276.9 %collective-permute-start.4 = (bf16[512,2048]{1,0:T(8,128)(2,1)}, bf16[512,2048]{1,0:T(8,128)(2,1)}, u32[]{:S(2)}, u32[]{:S(2)}) collective-permute-start(bf16[512,2048]{1,0:T(8,128)(2,1)} %pad_maximum_fusion), channel_id=1, source_target_pairs={{0,4},{4,0},{8,12},{12,8},{16,20},{20,16},{24,28},{28,24},{1,5},{5... | collective-permute-start | bytes 6291464 | tf_op jit(solution)/shard_map/ppermute | solution.py:37
  468.0 45.1 %collective-permute-done.4 = bf16[512,2048]{1,0:T(8,128)(2,1)} collective-permute-done((bf16[512,2048]{1,0:T(8,128)(2,1)}, bf16[512,2048]{1,0:T(8,128)(2,1)}, u32[]{:S(2)}, u32[]{:S(2)}) %collective-permute-start.4) | collective-permute-done | bytes 2097184 | tf_op jit(solution)/shard_map/ppermute | solution.py:37
  513.1 212.6 %collective-permute-done.6 = bf16[2048,3200]{0,1:T(8,128)(2,1)} collective-permute-done((bf16[2048,3200]{0,1:T(8,128)(2,1)}, bf16[2048,3200]{0,1:T(8,128)(2,1)}, u32[]{:S(2)}, u32[]{:S(2)}) %collective-permute-start.6) | collective-permute-done | bytes 13107232 | tf_op jit(solution)/shard_map/ppermute | solution.py:37
  725.7 49.2 %fusion = f32[1024,6400]{1,0:T(8,128)} fusion(bf16[2048,3200]{0,1:T(8,128)(2,1)} %maximum_select_fusion.2, bf16[2048,3200]{0,1:T(8,128)(2,1)} %collective-permute-done.6, pred[]{:T(512)S(6)} %eq.42, bf16[512,2048]{1,0:T(8,128)(2,1)} %collective-permute-done.4, bf16[256,2048]{1,0:T(8,128)(2,1)S(1)} %fusion.20, bf16[256,2048]{1,0:T(8,128)(2,1)S(1)} %bitcast.22), kind=kOutput, calls=%fused_computation.1 | convolution fusion | flops 26974093312 | bytes 56623104 | tf_op jit(solution)/shard_map/dot_general | solution.py:119
  774.8 9.4 %slice_reduce_fusion = (f32[512]{0:T(512)S(1)}, f32[512]{0:T(512)S(1)}) fusion(f32[1024,6400]{1,0:T(8,128)} %fusion), kind=kLoop, calls=%fused_computation.13 | loop fusion | flops 6552576 | bytes 26218496 | tf_op jit(solution)/shard_map/reduce_max | solution.py:47
  784.3 1.4 collective-permute-start.7
  785.7 5.1 copy-done
  790.8 6.9 exponential_reduce_fusion.1
  797.7 1.4 collective-permute-start.10
  800.6 0.8 collective-permute-done.10
  801.4 5.6 pmax.7
  807.0 6.6 all-reduce.1
  813.6 1.2 fusion.47
  814.8 88.0 %all-reduce = (f32[]{:T(128)}, f32[]{:T(128)}, f32[]{:T(128)}, f32[]{:T(128)}) all-reduce(f32[]{:T(128)} %get-tuple-element.25, f32[]{:T(128)} %get-tuple-element.27, f32[]{:T(128)} %get-tuple-element.19, f32[]{:T(128)} %get-tuple-element.17), channel_id=1, replica_groups=mesh['seq'=8,'vocab'=4] {'seq'}, use_global_device_ids=true, to_apply=%region_14.15 | all-reduce | flops 4 | bytes 32 | tf_op jit(solution)/shard_map/psum | solution.py:137
  (63 shorter events, 5.8 us)
Async XLA Ops:
  0.6 144.6 %collective-permute-start.5 = (bf16[2048,1600]{0,1:T(8,128)(2,1)}, bf16[2048,1600]{0,1:T(8,128)(2,1)}, u32[]{:S(2)}, u32[]{:S(2)}) collective-permute-start(bf16[2048,1600]{0,1:T(8,128)(2,1)} %param.18), channel_id=1, source_target_pairs={{0,8},{4,12},{8,0},{12,4},{16,24},{20,28},{24,16},{28,20},{1,9},{5... | collective-permute-start | bytes 19660808 | tf_op jit(solution)/shard_map/ppermute | solution.py:37
  3.7 159.8 %copy-start.1 = (bf16[2,128,2048]{2,1,0:T(8,128)(2,1)S(1)}, bf16[2,128,2048]{2,1,0:T(8,128)(2,1)}, u32[]{:S(2)}) copy-start(bf16[2,128,2048]{2,1,0:T(8,128)(2,1)} %param.12) | copy-start | bytes 3145732
  3.8 163.3 %copy-start.2 = (bf16[2,128,2048]{2,1,0:T(8,128)(2,1)S(1)}, bf16[2,128,2048]{2,1,0:T(8,128)(2,1)}, u32[]{:S(2)}) copy-start(bf16[2,128,2048]{2,1,0:T(8,128)(2,1)} %param.13) | copy-start | bytes 3145732
  3.8 163.6 %copy-start.3 = (f32[2048]{0:T(1024)S(1)}, f32[2048]{0:T(1024)}, u32[]{:S(2)}) copy-start(f32[2048]{0:T(1024)} %param.22) | copy-start | bytes 24580
  160.8 8.4 copy-start.4
  160.8 564.8 %collective-permute-start.6 = (bf16[2048,3200]{0,1:T(8,128)(2,1)}, bf16[2048,3200]{0,1:T(8,128)(2,1)}, u32[]{:S(2)}, u32[]{:S(2)}) collective-permute-start(bf16[2048,3200]{0,1:T(8,128)(2,1)} %maximum_select_fusion.2), channel_id=1, source_target_pairs={{0,16},{4,20},{8,24},{12,28},{16,0},{20,4},{24,8},{28,12},{1,17},{... | collective-permute-start | bytes 39321608 | tf_op jit(solution)/shard_map/ppermute | solution.py:37
  163.6 4.8 collective-permute-start
  167.6 2.2 copy-start.11
  169.8 12.9 %copy-start.5 = (f32[2048]{0:T(1024)S(1)}, f32[2048]{0:T(1024)}, u32[]{:S(2)}) copy-start(f32[2048]{0:T(1024)} %param.20) | copy-start | bytes 24580
  171.1 18.0 %copy-start.6 = (f32[2048]{0:T(1024)S(1)}, f32[2048]{0:T(1024)}, u32[]{:S(2)}) copy-start(f32[2048]{0:T(1024)} %param.23) | copy-start | bytes 24580
  171.1 5.8 collective-permute-start.1
  176.9 5.8 collective-permute-start.2
  182.7 5.8 collective-permute-start.3
  188.7 279.1 %copy-start.7 = (s32[2,128]{1,0:T(2,128)S(1)}, s32[2,128]{1,0:T(2,128)}, u32[]{:S(2)}) copy-start(s32[2,128]{1,0:T(2,128)} %param.14) | copy-start | bytes 3076
  190.9 322.2 %collective-permute-start.4 = (bf16[512,2048]{1,0:T(8,128)(2,1)}, bf16[512,2048]{1,0:T(8,128)(2,1)}, u32[]{:S(2)}, u32[]{:S(2)}) collective-permute-start(bf16[512,2048]{1,0:T(8,128)(2,1)} %pad_maximum_fusion), channel_id=1, source_target_pairs={{0,4},{4,0},{8,12},{12,8},{16,20},{20,16},{24,28},{28,24},{1,5},{5... | collective-permute-start | bytes 6291464 | tf_op jit(solution)/shard_map/ppermute | solution.py:37
  467.8 317.9 %collective-permute-start.9 = (s32[512]{0:T(512)S(1)}, s32[512]{0:T(512)S(1)}, u32[]{:S(2)}, u32[]{:S(2)}) collective-permute-start(s32[512]{0:T(512)S(1)} %pad_add_fusion), channel_id=1, source_target_pairs={{0,4},{4,0},{8,12},{12,8},{16,20},{20,16},{24,28},{28,24},{1,5},{5... | collective-permute-start | bytes 6152 | tf_op jit(solution)/shard_map/ppermute | solution.py:37
  774.8 16.0 %copy-start = (f32[1024,6400]{1,0:T(8,128)S(1)}, f32[1024,6400]{1,0:T(8,128)}, u32[]{:S(2)}) copy-start(f32[1024,6400]{1,0:T(8,128)} %fusion) | copy-start | bytes 78643200
  784.3 16.3 %collective-permute-start.7 = (f32[512]{0:T(512)S(1)}, f32[512]{0:T(512)S(1)}, u32[]{:S(2)}, u32[]{:S(2)}) collective-permute-start(f32[512]{0:T(512)S(1)} %get-tuple-element.9), channel_id=1, source_target_pairs={{0,4},{4,0},{8,12},{12,8},{16,20},{20,16},{24,28},{28,24},{1,5},{5... | collective-permute-start | bytes 6152 | tf_op jit(solution)/shard_map/ppermute | solution.py:37
  790.8 8.4 copy-start.8
  790.8 8.4 copy-start.9
  790.8 8.4 copy-start.10
  797.7 3.6 collective-permute-start.10
  799.9 7.1 collective-permute-start.8
